TPU v7x, 32 devices: a whole 2x2x4 slice. The times are simulated.
32 devices in a mesh: dp: 16 (over z, y, core), tensor: 2 (over x).
Axes of the slice: x: 2, y: 2, z: 4, core: 2. Of those that a mesh axis runs over, the one named last changes fastest.
Arguments:
- hidden_in: bfloat16 [2, 8192, 1024], P(None, ('dp', 'tensor')), may hold values from -6 to 6
- segment_ids: int32 [2, 16, 512], P(None, 'dp'), may hold values from 0 to 3, never falling along the last dimension, each value on 1 to 256 neighbouring positions
- out_grad: bfloat16 [2, 8192, 1024], P(None, ('dp', 'tensor')), may hold values from -6 to 6
- w_query: bfloat16 [1024, 1024], P(None, 'tensor'), may hold values from -0.1875 to 0.1875
- b_query: bfloat16 [1024], P('tensor'), may hold values from -1.75 to 1.75
- w_key: bfloat16 [1024, 1024], P(None, 'tensor'), may hold values from -0.1875 to 0.1875
- w_value: bfloat16 [1024, 1024], P(None, 'tensor'), may hold values from -0.1875 to 0.1875
- b_value: bfloat16 [1024], P('tensor'), may hold values from -1.75 to 1.75
- w_out: bfloat16 [1024, 1024], P('tensor'), may hold values from -0.75 to 0.75
- b_out: bfloat16 [1024], replicated, may hold values from -1.75 to 1.75
- attn_gain: bfloat16 [1024], replicated, may hold values from 0.099609375 to 1.8984375
- attn_shift: bfloat16 [1024], replicated, may hold values from -3 to 3
- w_up: bfloat16 [1024, 4096], P(None, 'tensor'), may hold values from -0.1875 to 0.1875
- b_up: bfloat16 [4096], P('tensor'), may hold values from -1.75 to 1.75
- w_down: bfloat16 [4096, 1024], P('tensor'), may hold values from -0.09375 to 0.09375
- b_down: bfloat16 [1024], replicated, may hold values from -1.75 to 1.75
- ffn_gain: bfloat16 [1024], replicated, may hold values from 0.099609375 to 1.8984375
- ffn_shift: bfloat16 [1024], replicated, may hold values from -3 to 3
Outputs:
- output: bfloat16 [2, 8192, 1024], P(None, ('dp', 'tensor'))
- grad_input: bfloat16 [2, 8192, 1024], P(None, ('dp', 'tensor'))
- grad_w_query: float32 [1024, 1024], P('dp', 'tensor')
- grad_b_query: float32 [1024], P('tensor')
- grad_w_key: float32 [1024, 1024], P('dp', 'tensor')
- grad_w_value: float32 [1024, 1024], P('dp', 'tensor')
- grad_b_value: float32 [1024], P('tensor')
- grad_w_out: float32 [1024, 1024], P('tensor', 'dp')
- grad_b_out: float32 [1024], replicated
- grad_attn_gain: float32 [1024], replicated
- grad_attn_shift: float32 [1024], replicated
- grad_w_up: float32 [1024, 4096], P('dp', 'tensor')
- grad_b_up: float32 [4096], P('tensor')
- grad_w_down: float32 [4096, 1024], P('tensor', 'dp')
- grad_b_down: float32 [1024], replicated
- grad_ffn_gain: float32 [1024], replicated
- grad_ffn_shift: float32 [1024], replicated
Inputs may be any that keep to these rules, and one draw needn't show every extreme that they name: `segment_ids`: along each packed row the ids never fall, every id from 0 to 3 occurs, and each covers 1 to 256 tokens; a token attends only to tokens of its own row with its own id.
All inputs are finite; a program needn't handle non-finite values.
Results may differ from a plain program's by a relative error of at most 0.02.
Values may be sent and summed in bfloat16 or wider, within the bound.
No kernel may reach another device: no remote copies, remote signals or barrier semaphores. Data moves between devices by JAX's collectives and lax.ppermute only.
A program may use at most 192 MiB of HBM per device.

v0:
```python
from functools import reduce
import math
import jax
import jax.numpy as jnp
from jax import lax
from jax.sharding import PartitionSpec as P

HD = 64
MICRO = 2


def layer_norm(inputs, scale_vec, offset):
    centre = inputs - jnp.mean(inputs, axis=-1, keepdims=True)
    spread = jnp.mean(centre * centre, axis=-1, keepdims=True)
    return centre * lax.rsqrt(spread + 1e-12) * scale_vec + offset


def gelu_exact(inputs):
    return jax.nn.gelu(inputs, approximate=False)


def matmul(former, latter):
    return jnp.dot(former, latter, preferred_element_type=jnp.float32)


def inner_rows(former, latter):
    return lax.dot_general(
        former, latter, (((0,), (0,)), ((), ())), preferred_element_type=jnp.float32
    )


def inner_cols(former, latter):
    return lax.dot_general(
        former, latter, (((1,), (1,)), ((), ())), preferred_element_type=jnp.float32
    )


def head_split(block):
    return block.reshape(block.shape[0], block.shape[1] // HD, HD)


def masked_scores(queries, key_rows, seg_row):
    scores = jnp.einsum(
        "qhd,khd->hqk",
        head_split(queries),
        head_split(key_rows),
        preferred_element_type=jnp.float32,
    ) * (1.0 / math.sqrt(HD))
    same_doc = seg_row[:, None] == seg_row[None, :]
    return jnp.where(same_doc[None], scores, -1e30)


def attend_row(packed):
    queries, key_rows, value_rows, seg_row = packed
    scores = masked_scores(queries, key_rows, seg_row)
    highest = jnp.max(scores, axis=-1, keepdims=True)
    logsum = highest + jnp.log(jnp.sum(jnp.exp(scores - highest), axis=-1, keepdims=True))
    probs_low = jnp.exp(scores - logsum).astype(jnp.bfloat16)
    context = jnp.einsum(
        "hqk,khd->qhd", probs_low, head_split(value_rows), preferred_element_type=jnp.float32
    )
    return (context.reshape(queries.shape).astype(jnp.bfloat16), logsum[..., 0])


def attend_back(packed):
    queries, key_rows, value_rows, seg_row, logsum, grad_ctx = packed
    scores = masked_scores(queries, key_rows, seg_row)
    probs = jnp.exp(scores - logsum[..., None])
    grad_heads = head_split(grad_ctx)
    grad_probs = jnp.einsum(
        "qhd,khd->hqk", grad_heads, head_split(value_rows), preferred_element_type=jnp.float32
    )
    centred = grad_probs - jnp.sum(probs * grad_probs, axis=-1, keepdims=True)
    grad_scores = (probs * centred * (1.0 / math.sqrt(HD))).astype(jnp.bfloat16)
    grad_query = jnp.einsum(
        "hqk,khd->qhd", grad_scores, head_split(key_rows), preferred_element_type=jnp.float32
    )
    grad_key = jnp.einsum(
        "hqk,qhd->khd", grad_scores, head_split(queries), preferred_element_type=jnp.float32
    )
    grad_value = jnp.einsum(
        "hqk,qhd->khd", probs.astype(jnp.bfloat16), grad_heads, preferred_element_type=jnp.float32
    )
    flat_shape = queries.shape
    return jnp.concatenate(
        [
            grad_query.reshape(flat_shape),
            grad_key.reshape(flat_shape),
            grad_value.reshape(flat_shape),
        ],
        axis=1,
    ).astype(jnp.bfloat16)


def add_trees(former, latter):
    return jax.tree.map(jnp.add, former, latter)


def on_device(
    hidden_in,
    segment_ids,
    out_grad,
    w_query,
    b_query,
    w_key,
    w_value,
    b_value,
    w_out,
    b_out,
    attn_gain,
    attn_shift,
    w_up,
    b_up,
    w_down,
    b_down,
    ffn_gain,
    ffn_shift,
):
    local_width = w_query.shape[1]
    packed_rows = segment_ids.shape[1]
    length = segment_ids.shape[2]
    w_qkv = jnp.concatenate([w_query, w_key, w_value], axis=1)
    b_qkv = jnp.concatenate([b_query, jnp.zeros_like(b_query), b_value]).astype(jnp.float32)
    b_out32 = b_out.astype(jnp.float32)
    b_up32 = b_up.astype(jnp.float32)
    b_down32 = b_down.astype(jnp.float32)
    attn_gain32 = attn_gain.astype(jnp.float32)
    attn_shift32 = attn_shift.astype(jnp.float32)
    ffn_gain32 = ffn_gain.astype(jnp.float32)
    ffn_shift32 = ffn_shift.astype(jnp.float32)

    def to_rows(block):
        return block.reshape(packed_rows, length, block.shape[1])

    outputs = []
    input_grads = []
    weight_terms = []
    small_terms = []
    for micro_step in range(MICRO):
        tokens_low = hidden_in[micro_step]
        tokens = tokens_low.astype(jnp.float32)
        seg_rows = segment_ids[micro_step]
        full_rows = lax.all_gather(tokens_low, "tensor", axis=0, tiled=True)
        qkv_low = (matmul(full_rows, w_qkv) + b_qkv).astype(jnp.bfloat16)
        queries = qkv_low[:, :local_width]
        key_rows = qkv_low[:, local_width : 2 * local_width]
        value_rows = qkv_low[:, 2 * local_width :]
        context, logsums = lax.map(
            attend_row, (to_rows(queries), to_rows(key_rows), to_rows(value_rows), seg_rows)
        )
        context = context.reshape(-1, local_width)
        attn_part = lax.psum_scatter(
            matmul(context, w_out).astype(jnp.bfloat16), "tensor", scatter_dimension=0, tiled=True
        ).astype(jnp.float32)
        resid_one = attn_part + b_out32 + tokens
        hidden_one, norm_one_back = jax.vjp(layer_norm, resid_one, attn_gain32, attn_shift32)
        hidden_low = hidden_one.astype(jnp.bfloat16)
        hidden_rows = lax.all_gather(hidden_low, "tensor", axis=0, tiled=True)
        pre_act = matmul(hidden_rows, w_up) + b_up32
        activation, gelu_back = jax.vjp(gelu_exact, pre_act)
        gelu_low = activation.astype(jnp.bfloat16)
        ffn_part = lax.psum_scatter(
            matmul(gelu_low, w_down).astype(jnp.bfloat16), "tensor", scatter_dimension=0, tiled=True
        ).astype(jnp.float32)
        resid_two = ffn_part + b_down32 + hidden_one
        result, norm_two_back = jax.vjp(layer_norm, resid_two, ffn_gain32, ffn_shift32)
        outputs.append(result.astype(jnp.bfloat16))
        grad_two, grad_ffn_gain, grad_ffn_shift = norm_two_back(
            out_grad[micro_step].astype(jnp.float32)
        )
        grad_two_low = grad_two.astype(jnp.bfloat16)
        grad_two_rows = lax.all_gather(grad_two_low, "tensor", axis=0, tiled=True)
        grad_down = inner_rows(gelu_low, grad_two_rows)
        grad_act = inner_cols(grad_two_rows, w_down)
        grad_pre = gelu_back(grad_act)[0].astype(jnp.bfloat16)
        grad_up = inner_rows(hidden_rows, grad_pre)
        grad_hidden = (
            lax.psum_scatter(
                inner_cols(grad_pre, w_up).astype(jnp.bfloat16),
                "tensor",
                scatter_dimension=0,
                tiled=True,
            ).astype(jnp.float32)
            + grad_two
        )
        grad_one, grad_attn_gain, grad_attn_shift = norm_one_back(grad_hidden)
        grad_one_low = grad_one.astype(jnp.bfloat16)
        grad_one_rows = lax.all_gather(grad_one_low, "tensor", axis=0, tiled=True)
        grad_wout = inner_rows(context, grad_one_rows)
        grad_ctx = inner_cols(grad_one_rows, w_out).astype(jnp.bfloat16)
        grad_qkv = lax.map(
            attend_back,
            (
                to_rows(queries),
                to_rows(key_rows),
                to_rows(value_rows),
                seg_rows,
                logsums,
                to_rows(grad_ctx),
            ),
        )
        grad_qkv = grad_qkv.reshape(-1, 3 * local_width)
        grad_wqkv = inner_rows(full_rows, grad_qkv)
        grad_in = (
            lax.psum_scatter(
                inner_cols(grad_qkv, w_qkv).astype(jnp.bfloat16),
                "tensor",
                scatter_dimension=0,
                tiled=True,
            ).astype(jnp.float32)
            + grad_one
        )
        input_grads.append(grad_in.astype(jnp.bfloat16))
        small_terms.append(
            (
                jnp.sum(grad_qkv.astype(jnp.float32), axis=0),
                jnp.sum(grad_pre.astype(jnp.float32), axis=0),
                jnp.sum(grad_one, axis=0),
                grad_attn_gain,
                grad_attn_shift,
                jnp.sum(grad_two, axis=0),
                grad_ffn_gain,
                grad_ffn_shift,
            )
        )
        weight_set = (grad_wqkv, grad_up, grad_wout, grad_down)
        weight_terms.append(weight_set)
    summed = reduce(add_trees, weight_terms)
    summed = (
        lax.psum_scatter(
            summed[0].astype(jnp.bfloat16), "dp", scatter_dimension=0, tiled=True
        ).astype(jnp.float32),
        lax.psum_scatter(
            summed[1].astype(jnp.bfloat16), "dp", scatter_dimension=0, tiled=True
        ).astype(jnp.float32),
        lax.psum_scatter(
            summed[2].astype(jnp.bfloat16), "dp", scatter_dimension=1, tiled=True
        ).astype(jnp.float32),
        lax.psum_scatter(
            summed[3].astype(jnp.bfloat16), "dp", scatter_dimension=1, tiled=True
        ).astype(jnp.float32),
    )
    red_qkv, red_up, red_wout, red_down = summed
    small = reduce(add_trees, small_terms)
    bias_qkv, bias_up = lax.psum((small[0], small[1]), "dp")
    norm_bout, norm_again, norm_ashift, norm_bdown, norm_fgain, norm_fshift = lax.psum(
        (small[2], small[3], small[4], small[5], small[6], small[7]), ("dp", "tensor")
    )
    output = jnp.stack(outputs, axis=0)
    grad_input = jnp.stack(input_grads, axis=0)
    return (
        output,
        grad_input,
        red_qkv[:, :local_width],
        bias_qkv[:local_width],
        red_qkv[:, local_width : 2 * local_width],
        red_qkv[:, 2 * local_width :],
        bias_qkv[2 * local_width :],
        red_wout,
        norm_bout,
        norm_again,
        norm_ashift,
        red_up,
        bias_up,
        red_down,
        norm_bdown,
        norm_fgain,
        norm_fshift,
    )


def solution(mesh):
    placed = (
        P(None, ("dp", "tensor"), None),
        P(None, "dp", None),
        P(None, ("dp", "tensor"), None),
        P(None, "tensor"),
        P("tensor"),
        P(None, "tensor"),
        P(None, "tensor"),
        P("tensor"),
        P("tensor", None),
        P(),
        P(),
        P(),
        P(None, "tensor"),
        P("tensor"),
        P("tensor", None),
        P(),
        P(),
        P(),
    )
    return jax.shard_map(
        on_device,
        mesh=mesh,
        in_specs=placed,
        out_specs=(
            P(None, ("dp", "tensor"), None),
            P(None, ("dp", "tensor"), None),
            P("dp", "tensor"),
            P("tensor"),
            P("dp", "tensor"),
            P("dp", "tensor"),
            P("tensor"),
            P("tensor", "dp"),
            P(),
            P(),
            P(),
            P("dp", "tensor"),
            P("tensor"),
            P("tensor", "dp"),
            P(),
            P(),
            P(),
        ),
        check_vma=False,
    )
```

profile of v0, /device:TPU:0, one launch (start us, length us, event | category | flops | bytes accessed | tf_op | source)
XLA Modules:
  0.0 747.1 jit_solution(17031704158051512009)
XLA Ops:
  14.8 19.4 %all-gather.25.cloned.1.call-done = bf16[1,512,1024]{2,1,0:T(8,128)(2,1)} async-done(((bf16[1,256,1024]{2,1,0:T(8,128)(2,1)}), bf16[1,512,1024]{2,1,0:T(8,128)(2,1)}) %all-gather.25.cloned.1.call-update) | async-done | bytes 1048592 | tf_op jit(solution)/shard_map/all_gather | solution.py:143
  34.2 4.1 fusion.71
  38.5 19.2 %all-gather.23.cloned.1.call-done = bf16[1,512,1024]{2,1,0:T(8,128)(2,1)} async-done(((bf16[1,256,1024]{2,1,0:T(8,128)(2,1)}), bf16[1,512,1024]{2,1,0:T(8,128)(2,1)}) %all-gather.23.cloned.1.call-update) | async-done | bytes 1048592 | tf_op jit(solution)/shard_map/all_gather | solution.py:143
  57.7 4.1 fusion.72
  81.6 10.4 %reduce-scatter.15.cloned.1.call-done = bf16[256,1024]{1,0:T(8,128)(2,1)} async-done(((bf16[512,1024]{1,0:T(8,128)(2,1)}), bf16[256,1024]{1,0:T(8,128)(2,1)}) %reduce-scatter.15.cloned.1.call-update) | async-done | bytes 524304 | tf_op jit(solution)/shard_map/reduce_scatter | solution.py:152
  93.5 21.7 %reduce-scatter.19.cloned.1.call-done = bf16[256,1024]{1,0:T(8,128)(2,1)} async-done(((bf16[512,1024]{1,0:T(8,128)(2,1)}), bf16[256,1024]{1,0:T(8,128)(2,1)}) %reduce-scatter.19.cloned.1.call-update) | async-done | bytes 524304 | tf_op jit(solution)/shard_map/reduce_scatter | solution.py:152
  118.3 2.6 fusion.106
  122.0 20.4 %all-gather.13.cloned.1.call-done = bf16[512,1024]{1,0:T(8,128)(2,1)} async-done(((bf16[256,1024]{1,0:T(8,128)(2,1)}), bf16[512,1024]{1,0:T(8,128)(2,1)}) %all-gather.13.cloned.1.call-update) | async-done | bytes 1048592 | tf_op jit(solution)/shard_map/all_gather | solution.py:158
  142.4 6.8 fusion.156
  149.1 16.5 %all-gather.11.cloned.1.call-done = bf16[512,1024]{1,0:T(8,128)(2,1)} async-done(((bf16[256,1024]{1,0:T(8,128)(2,1)}), bf16[512,1024]{1,0:T(8,128)(2,1)}) %all-gather.11.cloned.1.call-update) | async-done | bytes 1048592 | tf_op jit(solution)/shard_map/all_gather | solution.py:158
  165.7 24.0 %multiply_convert_fusion.3 = (bf16[512,2048]{1,0:T(8,128)(2,1)S(1)}, f32[512,2048]{1,0:T(8,128)}, bf16[512,2048]{1,0:T(8,128)(2,1)}, f32[512,2048]{1,0:T(8,128)}, f32[512,2048]{1,0:T(8,128)}) fusion(f32[2048]{0:T(1024)S(1)} %convert_element_type.251, f32[512,2048]{1,0:T(8,128)} %fusion.156, bf16[512,1024]{1,0:T(8,128)(2,1)} %all-gather.11.cloned.1.call-done, ...), kind=kOutput, calls=%fused_computation.48 | convolution fusion | flops 2285895680 | bytes 26222592 | tf_op jit(solution)/shard_map/dot_general | solution.py:23
  191.0 3.3 convolution_convert_fusion.7
  194.4 6.2 convolution_convert_fusion.6
  200.9 13.9 %reduce-scatter.17.cloned.1.call-done = bf16[256,1024]{1,0:T(8,128)(2,1)} async-done(((bf16[512,1024]{1,0:T(8,128)(2,1)}), bf16[256,1024]{1,0:T(8,128)(2,1)}) %reduce-scatter.17.cloned.1.call-update) | async-done | bytes 524304 | tf_op jit(solution)/shard_map/reduce_scatter | solution.py:162
  214.8 23.3 %reduce-scatter.21.cloned.1.call-done = bf16[256,1024]{1,0:T(8,128)(2,1)} async-done(((bf16[512,1024]{1,0:T(8,128)(2,1)}), bf16[256,1024]{1,0:T(8,128)(2,1)}) %reduce-scatter.21.cloned.1.call-update) | async-done | bytes 524304 | tf_op jit(solution)/shard_map/reduce_scatter | solution.py:162
  248.0 19.2 %all-gather.15.cloned.1.call-done = bf16[512,1024]{1,0:T(8,128)(2,1)} async-done(((bf16[256,1024]{1,0:T(8,128)(2,1)}), bf16[512,1024]{1,0:T(8,128)(2,1)}) %all-gather.15.cloned.1.call-update) | async-done | bytes 1048592 | tf_op jit(solution)/shard_map/all_gather | solution.py:172
  267.2 6.9 fusion.157
  274.1 15.8 %all-gather.19.cloned.1.call-done = bf16[512,1024]{1,0:T(8,128)(2,1)} async-done(((bf16[256,1024]{1,0:T(8,128)(2,1)}), bf16[512,1024]{1,0:T(8,128)(2,1)}) %all-gather.19.cloned.1.call-update) | async-done | bytes 1048592 | tf_op jit(solution)/shard_map/all_gather | solution.py:172
  289.9 13.2 %convert_reduce_fusion = (f32[2048]{0:T(1024)S(1)}, bf16[512,2048]{1,0:T(8,128)(2,1)S(1)}, f32[2048]{0:T(1024)S(1)}, bf16[512,2048]{1,0:T(8,128)(2,1)}) fusion(f32[512,2048]{1,0:T(8,128)} %get-tuple-element.221, f32[512,2048]{1,0:T(8,128)} %fusion.156, f32[2048]{0:T(1024)S(1)} %convert_element_type.251, f32[512,2048]{1,0:T(8,128)} %fusion.157, ...), kind=kOutput, calls=%fused_computation.29 | convolution fusion | flops 2183131136 | bytes 30433280 | tf_op jit(solution)/shard_map/dot_general | solution.py:33
  304.5 3.4 convolution_convert_fusion.4
  307.9 6.2 convolution_convert_fusion.5
  314.2 14.1 %reduce-scatter.27.cloned.1.call-done = bf16[256,1024]{1,0:T(8,128)(2,1)} async-done(((bf16[512,1024]{1,0:T(8,128)(2,1)}), bf16[256,1024]{1,0:T(8,128)(2,1)}) %reduce-scatter.27.cloned.1.call-update) | async-done | bytes 524304 | tf_op jit(solution)/shard_map/reduce_scatter | solution.py:178
  328.3 22.5 %reduce-scatter.23.cloned.1.call-done = bf16[256,1024]{1,0:T(8,128)(2,1)} async-done(((bf16[512,1024]{1,0:T(8,128)(2,1)}), bf16[256,1024]{1,0:T(8,128)(2,1)}) %reduce-scatter.23.cloned.1.call-update) | async-done | bytes 524304 | tf_op jit(solution)/shard_map/reduce_scatter | solution.py:178
  350.9 3.3 multiply_reduce_fusion.3
  360.7 19.2 %all-gather.17.cloned.1.call-done = bf16[512,1024]{1,0:T(8,128)(2,1)} async-done(((bf16[256,1024]{1,0:T(8,128)(2,1)}), bf16[512,1024]{1,0:T(8,128)(2,1)}) %all-gather.17.cloned.1.call-update) | async-done | bytes 1048592 | tf_op jit(solution)/shard_map/all_gather | solution.py:188
  382.0 21.2 %all-gather.21.cloned.1.call-done = bf16[512,1024]{1,0:T(8,128)(2,1)} async-done(((bf16[256,1024]{1,0:T(8,128)(2,1)}), bf16[512,1024]{1,0:T(8,128)(2,1)}) %all-gather.21.cloned.1.call-update) | async-done | bytes 1048592 | tf_op jit(solution)/shard_map/all_gather | solution.py:188
  403.1 3.1 add_convert_fusion.5
  409.5 4.5 fusion.158
  414.0 13.8 %fusion.83 = bf16[8,64,512]{2,1,0:T(8,128)(2,1)S(1)} fusion(bf16[512,8,64]{0,2,1:T(8,128)(2,1)S(1)} %bitcast.203, f32[8,512,512]{1,2,0:T(8,128)} %fusion.158, f32[8,512,512]{1,2,0:T(8,128)} %copy-done.3, f32[8,512]{1,0:T(8,128)S(1)} %log_add_fusion.1, pred[512,512]{0,1:T(8,128)(4,1)S(1)} %copy-done.14), kind=kOutput, calls=%fused_computation.115 | convolution fusion | flops 291770880 | bytes 18104320 | tf_op jit(solution)/shard_map/while/body/eval_jaxpr/hqk,khd->qhd/dot_general | solution.py:75
  427.8 14.5 %fusion.86 = bf16[8,64,512]{2,1,0:T(8,128)(2,1)} fusion(bf16[512,8,64]{0,2,1:T(8,128)(2,1)S(1)} %bitcast.201, f32[8,512,512]{1,2,0:T(8,128)} %fusion.158, f32[8,512,512]{1,2,0:T(8,128)} %copy-done.3, f32[8,512]{1,0:T(8,128)S(1)} %log_add_fusion.1, pred[512,512]{0,1:T(8,128)(4,1)S(1)} %copy-done.14), kind=kOutput, calls=%fused_computation.116 | convolution fusion | flops 291770880 | bytes 18104320 | tf_op jit(solution)/shard_map/while/body/eval_jaxpr/hqk,qhd->khd/dot_general | solution.py:78
  442.3 5.7 convolution_convert_fusion.9
  448.9 2.9 convolution_convert_fusion.1
  453.5 4.5 fusion.159
  458.0 13.3 %fusion.77 = bf16[8,64,512]{2,1,0:T(8,128)(2,1)S(1)} fusion(bf16[512,8,64]{0,2,1:T(8,128)(2,1)S(1)} %bitcast.197, f32[8,512,512]{1,2,0:T(8,128)} %fusion.159, f32[8,512,512]{1,2,0:T(8,128)} %copy-done.2, f32[8,512]{1,0:T(8,128)S(1)} %log_add_fusion, pred[512,512]{0,1:T(8,128)(4,1)S(1)} %broadcast_compare_fusion), kind=kOutput, calls=%fused_computation.113 | convolution fusion | flops 291770880 | bytes 18104320 | tf_op jit(solution)/shard_map/while/body/eval_jaxpr/hqk,khd->qhd/dot_general | solution.py:75
  471.4 13.6 %fusion.80 = bf16[8,64,512]{2,1,0:T(8,128)(2,1)S(1)} fusion(bf16[512,8,64]{0,2,1:T(8,128)(2,1)S(1)} %bitcast.195, f32[8,512,512]{1,2,0:T(8,128)} %fusion.159, f32[8,512,512]{1,2,0:T(8,128)} %copy-done.2, f32[8,512]{1,0:T(8,128)S(1)} %log_add_fusion, pred[512,512]{0,1:T(8,128)(4,1)S(1)} %broadcast_compare_fusion), kind=kOutput, calls=%fused_computation.114 | convolution fusion | flops 291770880 | bytes 18104320 | tf_op jit(solution)/shard_map/while/body/eval_jaxpr/hqk,qhd->khd/dot_general | solution.py:78
  485.1 5.9 convolution_convert_fusion.8
  491.0 2.9 convolution_convert_fusion
  494.2 4.5 fusion.161
  498.7 4.6 add_convert_fusion.1
  503.3 4.5 fusion.162
  507.9 4.7 add_convert_fusion
  512.9 3.5 fusion.99
  516.4 3.7 fusion.68
  520.1 4.8 copy.65
  527.7 40.6 %all-reduce = (f32[1024]{0:T(1024)}, f32[1024]{0:T(1024)}, f32[1024]{0:T(1024)}, f32[1024]{0:T(1024)}, f32[1024]{0:T(1024)}, /*index=5*/f32[1024]{0:T(1024)}) all-reduce(f32[1024]{0:T(1024)S(1)} %add.290, f32[1024]{0:T(1024)S(1)} %add.291, f32[1024]{0:T(1024)S(1)} %add.292, ...), channel_id=1, replica_groups=mesh['dp'=16,'tensor'=2] {'dp','tensor'}, use_global_device_ids=true, to_apply=%region_37.38 | all-reduce | flops 6144 | bytes 49152 | tf_op jit(solution)/shard_map/psum | solution.py:246
  571.7 60.7 %all-reduce.1 = (f32[1536]{0:T(1024)S(1)}, f32[2048]{0:T(1024)}) all-reduce(f32[1536]{0:T(1024)S(1)} %add.288, f32[2048]{0:T(1024)S(1)} %add.294), channel_id=1, replica_groups=mesh['dp'=16,'tensor'=2] {'dp'}, use_global_device_ids=true, to_apply=%region_33.34 | all-reduce | flops 3584 | bytes 28672 | tf_op jit(solution)/shard_map/psum | solution.py:245
  640.1 26.6 %reduce-scatter.35.cloned.1.call-done = bf16[2048,64]{0,1:T(8,128)(2,1)} async-done(((bf16[2048,1024]{0,1:T(8,128)(2,1)}), bf16[2048,64]{0,1:T(8,128)(2,1)}) %reduce-scatter.35.cloned.1.call-update) | async-done | bytes 262160 | tf_op jit(solution)/shard_map/reduce_scatter | solution.py:239
  668.5 67.8 %reduce-scatter.37.cloned.1.call-done = bf16[64,1536]{1,0:T(8,128)(2,1)} async-done(((bf16[1024,1536]{1,0:T(8,128)(2,1)}), bf16[64,1536]{1,0:T(8,128)(2,1)}) %reduce-scatter.37.cloned.1.call-update) | async-done | bytes 196624
  (255 shorter events, 79.8 us)
Async XLA Ops:
  7.2 62.7 %copy-start = (bf16[512,1024]{1,0:T(8,128)(2,1)S(1)}, bf16[512,1024]{1,0:T(8,128)(2,1)}, u32[]{:S(2)}) copy-start(bf16[512,1024]{1,0:T(8,128)(2,1)} %param.26) | copy-start | bytes 3145732
  7.2 5.6 copy-start.33
  7.2 5.7 copy-start.34
  7.2 27.0 %all-gather.25.cloned.1.call-start = ((), (), s32[]{:S(2)}) async-start(), calls=%async_computation.30 | async-start | bytes 1572864 | tf_op jit(solution)/shard_map/all_gather | solution.py:143
  9.7 48.0 %all-gather.23.cloned.1.call-start = ((), (), s32[]{:S(2)}) async-start(), calls=%async_computation.29 | async-start | bytes 1572864 | tf_op jit(solution)/shard_map/all_gather | solution.py:143
  10.4 81.6 %reduce-scatter.15.cloned.1.call-start = ((), (), s32[]{:S(2)}) async-start(), calls=%async_computation.12 | async-start | bytes 1572864 | tf_op jit(solution)/shard_map/reduce_scatter | solution.py:152
  11.4 53.8 %copy-start.13 = (pred[512,512]{0,1:T(8,128)(4,1)}, pred[512,512]{0,1:T(8,128)(4,1)S(1)}, u32[]{:S(2)}) copy-start(pred[512,512]{0,1:T(8,128)(4,1)S(1)} %broadcast_compare_fusion.1) | copy-start | bytes 786436
  38.5 33.4 %copy-start.18 = (bf16[512,512]{0,1:T(8,128)(2,1)}, bf16[512,512]{0,1:T(8,128)(2,1)S(1)}, u32[]{:S(2)}) copy-start(bf16[512,512]{0,1:T(8,128)(2,1)S(1)} %get-tuple-element.190) | copy-start | bytes 1572868
  38.5 33.4 %copy-start.20 = (bf16[512,512]{0,1:T(8,128)(2,1)}, bf16[512,512]{0,1:T(8,128)(2,1)S(1)}, u32[]{:S(2)}) copy-start(bf16[512,512]{0,1:T(8,128)(2,1)S(1)} %get-tuple-element.189) | copy-start | bytes 1572868
  38.5 36.7 %copy-start.22 = (bf16[512,512]{0,1:T(8,128)(2,1)}, bf16[512,512]{0,1:T(8,128)(2,1)S(1)}, u32[]{:S(2)}) copy-start(bf16[512,512]{0,1:T(8,128)(2,1)S(1)} %get-tuple-element.191) | copy-start | bytes 1572868
  71.6 43.6 %reduce-scatter.19.cloned.1.call-start = ((), (), s32[]{:S(2)}) async-start(), calls=%async_computation.15 | async-start | bytes 1572864 | tf_op jit(solution)/shard_map/reduce_scatter | solution.py:152
  76.6 5.0 copy-start.50
  79.0 13.1 %copy-start.1 = (bf16[2,256,1024]{2,1,0:T(8,128)(2,1)S(1)}, bf16[2,256,1024]{2,1,0:T(8,128)(2,1)}, u32[]{:S(2)}) copy-start(bf16[2,256,1024]{2,1,0:T(8,128)(2,1)} %param.18) | copy-start | bytes 3145732
  81.5 60.8 %all-gather.13.cloned.1.call-start = ((), (), s32[]{:S(2)}) async-start(), calls=%async_computation.16 | async-start | bytes 1572864 | tf_op jit(solution)/shard_map/all_gather | solution.py:158
  81.6 40.3 %copy-start.47 = (bf16[2048]{0:T(1024)(128)(2,1)S(1)}, bf16[2048]{0:T(1024)(128)(2,1)}, u32[]{:S(2)}) copy-start(bf16[2048]{0:T(1024)(128)(2,1)} %param.31) | copy-start | bytes 12292
  92.1 26.2 %copy-start.4 = (bf16[256,1024]{1,0:T(8,128)(2,1)S(1)}, bf16[256,1024]{1,0:T(8,128)(2,1)}, u32[]{:S(2)}) copy-start(bf16[256,1024]{1,0:T(8,128)(2,1)} %reduce-scatter.15.cloned.1.call-done) | copy-start | bytes 1572868
  120.9 44.8 %all-gather.11.cloned.1.call-start = ((), (), s32[]{:S(2)}) async-start(), calls=%async_computation.13 | async-start | bytes 1572864 | tf_op jit(solution)/shard_map/all_gather | solution.py:158
  121.5 93.3 %reduce-scatter.17.cloned.1.call-start = ((), (), s32[]{:S(2)}) async-start(), calls=%async_computation.14 | async-start | bytes 1572864 | tf_op jit(solution)/shard_map/reduce_scatter | solution.py:162
  165.7 25.3 %copy-start.56 = (bf16[2048,1024]{1,0:T(8,128)(2,1)S(1)}, bf16[2048,1024]{1,0:T(8,128)(2,1)}, u32[]{:S(2)}) copy-start(bf16[2048,1024]{1,0:T(8,128)(2,1)} %param.32) | copy-start | bytes 12582916
  194.3 43.7 %reduce-scatter.21.cloned.1.call-start = ((), (), s32[]{:S(2)}) async-start(), calls=%async_computation.17 | async-start | bytes 1572864 | tf_op jit(solution)/shard_map/reduce_scatter | solution.py:162
  194.4 6.5 copy-start.51
  194.4 6.5 copy-start.52
  194.4 6.5 copy-start.53
  194.4 43.6 %copy-start.5 = (bf16[256,1024]{1,0:T(8,128)(2,1)S(1)}, bf16[256,1024]{1,0:T(8,128)(2,1)}, u32[]{:S(2)}) copy-start(bf16[256,1024]{1,0:T(8,128)(2,1)} %reduce-scatter.19.cloned.1.call-done) | copy-start | bytes 1572868
  200.6 66.5 %all-gather.15.cloned.1.call-start = ((), (), s32[]{:S(2)}) async-start(), calls=%async_computation.18 | async-start | bytes 1572864 | tf_op jit(solution)/shard_map/all_gather | solution.py:172
  245.7 44.2 %all-gather.19.cloned.1.call-start = ((), (), s32[]{:S(2)}) async-start(), calls=%async_computation.22 | async-start | bytes 1572864 | tf_op jit(solution)/shard_map/all_gather | solution.py:172
  247.9 80.4 %reduce-scatter.27.cloned.1.call-start = ((), (), s32[]{:S(2)}) async-start(), calls=%async_computation.23 | async-start | bytes 1572864 | tf_op jit(solution)/shard_map/reduce_scatter | solution.py:178
  289.9 14.6 %copy-start.57 = (bf16[1024,2048]{1,0:T(8,128)(2,1)S(1)}, bf16[1024,2048]{1,0:T(8,128)(2,1)}, u32[]{:S(2)}) copy-start(bf16[1024,2048]{1,0:T(8,128)(2,1)} %param.30) | copy-start | bytes 12582916
  307.9 43.0 %reduce-scatter.23.cloned.1.call-start = ((), (), s32[]{:S(2)}) async-start(), calls=%async_computation.19 | async-start | bytes 1572864 | tf_op jit(solution)/shard_map/reduce_scatter | solution.py:178
  314.2 65.7 %all-gather.17.cloned.1.call-start = ((), (), s32[]{:S(2)}) async-start(), calls=%async_computation.20 | async-start | bytes 1572864 | tf_op jit(solution)/shard_map/all_gather | solution.py:188
  358.4 44.8 %all-gather.21.cloned.1.call-start = ((), (), s32[]{:S(2)}) async-start(), calls=%async_computation.24 | async-start | bytes 1572864 | tf_op jit(solution)/shard_map/all_gather | solution.py:188
  360.6 272.3 %reduce-scatter.31.cloned.1.call-start = ((), (), s32[]{:S(2)}) async-start(), calls=%async_computation.26 | async-start | bytes 1114112 | tf_op jit(solution)/shard_map/reduce_scatter | solution.py:236
  406.3 228.2 %reduce-scatter.25.cloned.1.call-start = ((), (), s32[]{:S(2)}) async-start(), calls=%async_computation.21 | async-start | bytes 1572864 | tf_op jit(solution)/shard_map/reduce_scatter | solution.py:205
  414.0 13.8 %copy-start.25 = (bf16[512,512]{0,1:T(8,128)(2,1)S(1)}, bf16[512,512]{0,1:T(8,128)(2,1)}, u32[]{:S(2)}) copy-start(bf16[512,512]{0,1:T(8,128)(2,1)} %copy-done.24) | copy-start | bytes 1572868
  427.8 85.1 %copy-start.38 = (bf16[8,64,512]{2,1,0:T(8,128)(2,1)}, bf16[8,64,512]{2,1,0:T(8,128)(2,1)S(1)}, u32[]{:S(2)}) copy-start(bf16[8,64,512]{2,1,0:T(8,128)(2,1)S(1)} %fusion.83) | copy-start | bytes 1572868
  427.8 14.5 %copy-start.42 = (bf16[512,512]{0,1:T(8,128)(2,1)S(1)}, bf16[512,512]{0,1:T(8,128)(2,1)}, u32[]{:S(2)}) copy-start(bf16[512,512]{0,1:T(8,128)(2,1)} %copy-done.41) | copy-start | bytes 1572868
  442.3 6.6 copy-start.39
  442.3 6.6 copy-start.45
  451.8 184.3 %reduce-scatter.29.cloned.1.call-start = ((), (), s32[]{:S(2)}) async-start(), calls=%async_computation.25 | async-start | bytes 1572864 | tf_op jit(solution)/shard_map/reduce_scatter | solution.py:205
  458.0 13.3 %copy-start.19 = (bf16[512,512]{0,1:T(8,128)(2,1)S(1)}, bf16[512,512]{0,1:T(8,128)(2,1)}, u32[]{:S(2)}) copy-start(bf16[512,512]{0,1:T(8,128)(2,1)} %copy-done.18) | copy-start | bytes 1572868
  471.4 45.0 %copy-start.15 = (bf16[8,64,512]{2,1,0:T(8,128)(2,1)}, bf16[8,64,512]{2,1,0:T(8,128)(2,1)S(1)}, u32[]{:S(2)}) copy-start(bf16[8,64,512]{2,1,0:T(8,128)(2,1)S(1)} %fusion.77) | copy-start | bytes 1572868
  485.1 31.4 %copy-start.16 = (bf16[8,64,512]{2,1,0:T(8,128)(2,1)}, bf16[8,64,512]{2,1,0:T(8,128)(2,1)S(1)}, u32[]{:S(2)}) copy-start(bf16[8,64,512]{2,1,0:T(8,128)(2,1)S(1)} %fusion.80) | copy-start | bytes 1572868
  485.1 5.9 copy-start.46
  491.0 25.4 %copy-start.17 = (bf16[8,64,512]{2,1,0:T(8,128)(2,1)}, bf16[8,64,512]{2,1,0:T(8,128)(2,1)S(1)}, u32[]{:S(2)}) copy-start(bf16[8,64,512]{2,1,0:T(8,128)(2,1)S(1)} %convolution_convert_fusion.8) | copy-start | bytes 1572868
  493.9 144.4 %reduce-scatter.33.cloned.1.call-start = ((), (), s32[]{:S(2)}) async-start(), calls=%async_computation.27 | async-start | bytes 4456448 | tf_op jit(solution)/shard_map/reduce_scatter | solution.py:233
  503.3 163.5 %reduce-scatter.35.cloned.1.call-start = ((), (), s32[]{:S(2)}) async-start(), calls=%async_computation.28 | async-start | bytes 4456448 | tf_op jit(solution)/shard_map/reduce_scatter | solution.py:239
  512.6 223.7 %reduce-scatter.37.cloned.1.call-start = ((), (), s32[]{:S(2)}) async-start(), calls=%async_computation.31 | async-start | bytes 3342336
  525.0 111.1 %copy-start.11 = (f32[256,1024]{1,0:T(8,128)S(1)}, f32[256,1024]{1,0:T(8,128)}, u32[]{:S(2)}) copy-start(f32[256,1024]{1,0:T(8,128)} %get-tuple-element.200) | copy-start | bytes 3145732
  (36 other events, 104.2 us)
Sparse Core Ops, SparseCore 0:
  10.2 23.9 all-gather.24
  36.3 21.2 all-gather.22
  71.7 20.3 reduce-scatter.14
  94.8 20.3 reduce-scatter.18
  121.0 21.2 all-gather.12
  144.3 21.2 all-gather.10
  194.5 20.3 reduce-scatter.16
  217.7 20.3 reduce-scatter.20
  245.8 21.2 all-gather.14
  268.6 21.2 all-gather.18
  308.0 20.3 reduce-scatter.26
  330.5 20.3 reduce-scatter.22
  358.5 21.2 all-gather.16
  381.8 21.2 all-gather.20
  406.6 57.3 reduce-scatter.30
  466.2 19.3 reduce-scatter.24
  494.0 20.5 reduce-scatter.28
  518.9 72.6 reduce-scatter.32
  595.4 71.3 reduce-scatter.34
  670.9 65.3 reduce-scatter.36
where the time goes:
time: 756 us; the launch traced here: 747 us
  waiting for transfers between devices  353 us (47%)
  matrix products  204 us (27%)
  blocking collectives  101 us (13%)
  other arithmetic  43.3 us (6%)
  local copies, waits for them, and re-layouts  27.1 us (4%)
  between operations  15.8 us (2%)
    unnamed x21, waiting for transfers between devices  69.3 us
    psum x1, blocking collectives, on_device(): bias_qkv, bias_up = lax.psum((small[0], small[1]), 'dp')  60.7 us
    dot_general x8, matrix products, matmul(): return jnp.dot(former, latter, preferred_element_type=jnp.float32)  51.9 us
    psum x1, blocking collectives, on_device(): lax.psum((small[2], small[3], small[4], small[5], small[6], small[7]), ('...  40.6 us
    all_gather x2, waiting for transfers between devices, on_device(): grad_one_rows = lax.all_gather(grad_one_low, 'tensor', axis=0, tiled=True)  40.3 us
    all_gather x2, waiting for transfers between devices, on_device(): full_rows = lax.all_gather(tokens_low, 'tensor', axis=0, tiled=True)  38.6 us
    dot_general x8, matrix products, inner_cols(): lax.dot_general(former, latter, (((1,), (1,)), ((), ())), preferred_eleme...  38.1 us
    reduce_scatter x2, waiting for transfers between devices, on_device(): lax.psum_scatter(matmul(gelu_low, w_down).astype(jnp.bfloat16), 'tensor',...  37.1 us
  transfers between devices with their start and end apart: 20, of which 16 were waited for; matrix products, arithmetic and copies ran while one was open for 24% of the time, Pallas kernels for 0%

commit v1 on v0

--- a/solution.py
+++ b/solution.py
@@ -140,7 +140,21 @@
         tokens_low = hidden_in[micro_step]
         tokens = tokens_low.astype(jnp.float32)
         seg_rows = segment_ids[micro_step]
-        full_rows = lax.all_gather(tokens_low, "tensor", axis=0, tiled=True)
+        frame_out = lax.axis_index("tensor")
+        b_next = lax.axis_size("tensor")
+        low, mixed_arr = (b_next, frame_out)
+        full_rows, n_now = (tokens_low, 1)
+        while n_now < low:
+            steps_seen = []
+            ix = 0
+            while ix < low:
+                steps_seen.append((ix, ix ^ n_now))
+                ix += 1
+            w2 = lax.ppermute(full_rows, axis_name="tensor", perm=steps_seen)
+            val = jnp.concatenate([full_rows, w2], 0)
+            far_arr = jnp.concatenate([w2, full_rows], 0)
+            full_rows = jnp.where(mixed_arr & n_now == 0, val, far_arr)
+            n_now = 2 * n_now
         qkv_low = (matmul(full_rows, w_qkv) + b_qkv).astype(jnp.bfloat16)
         queries = qkv_low[:, :local_width]
         key_rows = qkv_low[:, local_width : 2 * local_width]

time: 756 us -> 742 us (0.981)
  waiting for transfers between devices: 353 us -> 326 us
    unnamed x21 -> x18, waiting for transfers between devices: 69.3 us -> 0.8 us
    reduce_scatter x0 -> x1, waiting for transfers between devices: none -> 67.7 us  [on_device(): lax.psum_scatter(summed[0].astype(jnp.bfloat16), 'dp', scatter_dimension=...]
    all_gather x2 -> x0, waiting for transfers between devices: 38.6 us -> none  [on_device(): full_rows = lax.all_gather(tokens_low, 'tensor', axis=0, tiled=True)]
    ppermute x0 -> x2, waiting for transfers between devices: none -> 10.6 us  [on_device(): w2 = lax.ppermute(full_rows, axis_name='tensor', perm=steps_seen)]
    unnamed x135 -> x132, local copies, waits for them, and re-layouts: 23.1 us -> 16.4 us
  transfers between devices with their start and end apart: 20 -> 20, of which waited for: 16 -> 16; matrix products, arithmetic and copies ran while one was open for 24% -> 25% of each run, Pallas kernels for 0% -> 0%
where the time goes in v1:
time: 742 us; the launch traced here: 733 us
  waiting for transfers between devices  326 us (44%)
  matrix products  208 us (28%)
  blocking collectives  102 us (14%)
  other arithmetic  43.1 us (6%)
  local copies, waits for them, and re-layouts  32.9 us (4%)
  between operations  15.7 us (2%)
    reduce_scatter x1, waiting for transfers between devices, on_device(): lax.psum_scatter(summed[0].astype(jnp.bfloat16), 'dp', scatter_dimension=...  67.7 us
    psum x1, blocking collectives, on_device(): bias_qkv, bias_up = lax.psum((small[0], small[1]), 'dp')  61.2 us
    dot_general x8, matrix products, matmul(): return jnp.dot(former, latter, preferred_element_type=jnp.float32)  52.3 us
    psum x1, blocking collectives, on_device(): lax.psum((small[2], small[3], small[4], small[5], small[6], small[7]), ('...  40.9 us
    all_gather x2, waiting for transfers between devices, on_device(): grad_one_rows = lax.all_gather(grad_one_low, 'tensor', axis=0, tiled=True)  40.3 us
    dot_general x8, matrix products, inner_cols(): lax.dot_general(former, latter, (((1,), (1,)), ((), ())), preferred_eleme...  38.1 us
    reduce_scatter x2, waiting for transfers between devices, on_device(): lax.psum_scatter(matmul(gelu_low, w_down).astype(jnp.bfloat16), 'tensor',...  37 us
    all_gather x2, waiting for transfers between devices, on_device(): hidden_rows = lax.all_gather(hidden_low, 'tensor', axis=0, tiled=True)  37 us
  transfers between devices with their start and end apart: 20, of which 16 were waited for; matrix products, arithmetic and copies ran while one was open for 25% of the time, Pallas kernels for 0%

profile of v1, /device:TPU:0, one launch (start us, length us, event | category | flops | bytes accessed | tf_op | source)
XLA Modules:
  0.0 733.4 jit_solution(10031405647437568592)
XLA Ops:
  9.7 2.9 collective-permute-start.1
  18.4 7.3 collective-permute-done.1
  25.7 4.3 fusion.69
  32.8 3.2 collective-permute-done
  36.1 4.3 fusion.68
  47.7 2.7 fusion.4
  68.6 11.9 %reduce-scatter.13.cloned.1.call-done = bf16[256,1024]{1,0:T(8,128)(2,1)} async-done(((bf16[512,1024]{1,0:T(8,128)(2,1)}), bf16[256,1024]{1,0:T(8,128)(2,1)}) %reduce-scatter.13.cloned.1.call-update) | async-done | bytes 524304 | tf_op jit(solution)/shard_map/reduce_scatter | solution.py:166
  81.9 21.9 %reduce-scatter.17.cloned.1.call-done = bf16[256,1024]{1,0:T(8,128)(2,1)} async-done(((bf16[512,1024]{1,0:T(8,128)(2,1)}), bf16[256,1024]{1,0:T(8,128)(2,1)}) %reduce-scatter.17.cloned.1.call-update) | async-done | bytes 524304 | tf_op jit(solution)/shard_map/reduce_scatter | solution.py:166
  110.5 20.4 %all-gather.9.cloned.1.call-done = bf16[512,1024]{1,0:T(8,128)(2,1)} async-done(((bf16[256,1024]{1,0:T(8,128)(2,1)}), bf16[512,1024]{1,0:T(8,128)(2,1)}) %all-gather.9.cloned.1.call-update) | async-done | bytes 1048592 | tf_op jit(solution)/shard_map/all_gather | solution.py:172
  130.9 6.8 fusion.152
  137.7 16.5 %all-gather.7.cloned.1.call-done = bf16[512,1024]{1,0:T(8,128)(2,1)} async-done(((bf16[256,1024]{1,0:T(8,128)(2,1)}), bf16[512,1024]{1,0:T(8,128)(2,1)}) %all-gather.7.cloned.1.call-update) | async-done | bytes 1048592 | tf_op jit(solution)/shard_map/all_gather | solution.py:172
  154.3 24.0 %multiply_convert_fusion.3 = (bf16[512,2048]{1,0:T(8,128)(2,1)S(1)}, f32[512,2048]{1,0:T(8,128)}, bf16[512,2048]{1,0:T(8,128)(2,1)}, f32[512,2048]{1,0:T(8,128)}, f32[512,2048]{1,0:T(8,128)}) fusion(f32[2048]{0:T(1024)S(1)} %convert_element_type.241, f32[512,2048]{1,0:T(8,128)} %fusion.152, bf16[512,1024]{1,0:T(8,128)(2,1)} %all-gather.7.cloned.1.call-done, ...), kind=kOutput, calls=%fused_computation.48 | convolution fusion | flops 2285895680 | bytes 26222592 | tf_op jit(solution)/shard_map/dot_general | solution.py:23
  179.6 3.3 convolution_convert_fusion.7
  183.0 6.2 convolution_convert_fusion.6
  189.5 13.9 %reduce-scatter.15.cloned.1.call-done = bf16[256,1024]{1,0:T(8,128)(2,1)} async-done(((bf16[512,1024]{1,0:T(8,128)(2,1)}), bf16[256,1024]{1,0:T(8,128)(2,1)}) %reduce-scatter.15.cloned.1.call-update) | async-done | bytes 524304 | tf_op jit(solution)/shard_map/reduce_scatter | solution.py:176
  203.4 23.1 %reduce-scatter.19.cloned.1.call-done = bf16[256,1024]{1,0:T(8,128)(2,1)} async-done(((bf16[512,1024]{1,0:T(8,128)(2,1)}), bf16[256,1024]{1,0:T(8,128)(2,1)}) %reduce-scatter.19.cloned.1.call-update) | async-done | bytes 524304 | tf_op jit(solution)/shard_map/reduce_scatter | solution.py:176
  236.4 19.2 %all-gather.11.cloned.1.call-done = bf16[512,1024]{1,0:T(8,128)(2,1)} async-done(((bf16[256,1024]{1,0:T(8,128)(2,1)}), bf16[512,1024]{1,0:T(8,128)(2,1)}) %all-gather.11.cloned.1.call-update) | async-done | bytes 1048592 | tf_op jit(solution)/shard_map/all_gather | solution.py:186
  255.6 6.9 fusion.153
  262.5 16.0 %all-gather.15.cloned.1.call-done = bf16[512,1024]{1,0:T(8,128)(2,1)} async-done(((bf16[256,1024]{1,0:T(8,128)(2,1)}), bf16[512,1024]{1,0:T(8,128)(2,1)}) %all-gather.15.cloned.1.call-update) | async-done | bytes 1048592 | tf_op jit(solution)/shard_map/all_gather | solution.py:186
  278.5 13.2 %convert_reduce_fusion = (f32[2048]{0:T(1024)S(1)}, bf16[512,2048]{1,0:T(8,128)(2,1)S(1)}, f32[2048]{0:T(1024)S(1)}, bf16[512,2048]{1,0:T(8,128)(2,1)}) fusion(f32[512,2048]{1,0:T(8,128)} %get-tuple-element.187, f32[512,2048]{1,0:T(8,128)} %fusion.152, f32[2048]{0:T(1024)S(1)} %convert_element_type.241, f32[512,2048]{1,0:T(8,128)} %fusion.153, ...), kind=kOutput, calls=%fused_computation.29 | convolution fusion | flops 2183131136 | bytes 30433280 | tf_op jit(solution)/shard_map/dot_general | solution.py:33
  293.1 3.4 convolution_convert_fusion.4
  296.5 6.2 convolution_convert_fusion.5
  302.8 14.1 %reduce-scatter.25.cloned.1.call-done = bf16[256,1024]{1,0:T(8,128)(2,1)} async-done(((bf16[512,1024]{1,0:T(8,128)(2,1)}), bf16[256,1024]{1,0:T(8,128)(2,1)}) %reduce-scatter.25.cloned.1.call-update) | async-done | bytes 524304 | tf_op jit(solution)/shard_map/reduce_scatter | solution.py:192
  316.9 22.5 %reduce-scatter.21.cloned.1.call-done = bf16[256,1024]{1,0:T(8,128)(2,1)} async-done(((bf16[512,1024]{1,0:T(8,128)(2,1)}), bf16[256,1024]{1,0:T(8,128)(2,1)}) %reduce-scatter.21.cloned.1.call-update) | async-done | bytes 524304 | tf_op jit(solution)/shard_map/reduce_scatter | solution.py:192
  339.5 3.3 multiply_reduce_fusion.3
  349.3 19.2 %all-gather.13.cloned.1.call-done = bf16[512,1024]{1,0:T(8,128)(2,1)} async-done(((bf16[256,1024]{1,0:T(8,128)(2,1)}), bf16[512,1024]{1,0:T(8,128)(2,1)}) %all-gather.13.cloned.1.call-update) | async-done | bytes 1048592 | tf_op jit(solution)/shard_map/all_gather | solution.py:202
  370.6 21.2 %all-gather.17.cloned.1.call-done = bf16[512,1024]{1,0:T(8,128)(2,1)} async-done(((bf16[256,1024]{1,0:T(8,128)(2,1)}), bf16[512,1024]{1,0:T(8,128)(2,1)}) %all-gather.17.cloned.1.call-update) | async-done | bytes 1048592 | tf_op jit(solution)/shard_map/all_gather | solution.py:202
  391.7 3.1 add_convert_fusion.5
  397.3 4.5 fusion.154
  401.8 14.6 %fusion.80 = bf16[8,64,512]{2,1,0:T(8,128)(2,1)} fusion(bf16[512,8,64]{0,2,1:T(8,128)(2,1)S(1)} %bitcast.179, f32[8,512,512]{1,2,0:T(8,128)} %fusion.154, f32[8,512,512]{1,2,0:T(8,128)} %copy-done.3, f32[8,512]{1,0:T(8,128)S(1)} %log_add_fusion.1, pred[512,512]{0,1:T(8,128)(4,1)S(1)} %copy-done.14), kind=kOutput, calls=%fused_computation.112 | convolution fusion | flops 291770880 | bytes 18104320 | tf_op jit(solution)/shard_map/while/body/eval_jaxpr/hqk,khd->qhd/dot_general | solution.py:75
  416.4 14.3 %fusion.83 = bf16[8,64,512]{2,1,0:T(8,128)(2,1)} fusion(bf16[512,8,64]{0,2,1:T(8,128)(2,1)S(1)} %bitcast.181, f32[8,512,512]{1,2,0:T(8,128)} %fusion.154, f32[8,512,512]{1,2,0:T(8,128)} %copy-done.3, f32[8,512]{1,0:T(8,128)S(1)} %log_add_fusion.1, pred[512,512]{0,1:T(8,128)(4,1)S(1)} %copy-done.14), kind=kOutput, calls=%fused_computation.113 | convolution fusion | flops 291770880 | bytes 18104320 | tf_op jit(solution)/shard_map/while/body/eval_jaxpr/hqk,qhd->khd/dot_general | solution.py:78
  430.7 5.7 convolution_convert_fusion.9
  437.3 2.8 convolution_convert_fusion.1
  442.0 4.5 fusion.155
  446.5 13.3 %fusion.74 = bf16[8,64,512]{2,1,0:T(8,128)(2,1)S(1)} fusion(bf16[512,8,64]{0,2,1:T(8,128)(2,1)S(1)} %bitcast.173, f32[8,512,512]{1,2,0:T(8,128)} %fusion.155, f32[8,512,512]{1,2,0:T(8,128)} %copy-done.2, f32[8,512]{1,0:T(8,128)S(1)} %log_add_fusion, pred[512,512]{0,1:T(8,128)(4,1)S(1)} %broadcast_compare_fusion), kind=kOutput, calls=%fused_computation.110 | convolution fusion | flops 291770880 | bytes 18104320 | tf_op jit(solution)/shard_map/while/body/eval_jaxpr/hqk,khd->qhd/dot_general | solution.py:75
  459.8 13.7 %fusion.77 = bf16[8,64,512]{2,1,0:T(8,128)(2,1)S(1)} fusion(bf16[512,8,64]{0,2,1:T(8,128)(2,1)S(1)} %bitcast.175, f32[8,512,512]{1,2,0:T(8,128)} %fusion.155, f32[8,512,512]{1,2,0:T(8,128)} %copy-done.2, f32[8,512]{1,0:T(8,128)S(1)} %log_add_fusion, pred[512,512]{0,1:T(8,128)(4,1)S(1)} %broadcast_compare_fusion), kind=kOutput, calls=%fused_computation.111 | convolution fusion | flops 291770880 | bytes 18104320 | tf_op jit(solution)/shard_map/while/body/eval_jaxpr/hqk,qhd->khd/dot_general | solution.py:78
  473.5 5.8 convolution_convert_fusion.8
  479.4 2.8 convolution_convert_fusion
  482.5 4.5 fusion.157
  487.0 4.6 add_convert_fusion.1
  492.8 4.2 fusion.158
  497.1 4.7 add_convert_fusion
  503.0 3.6 fusion.104
  506.6 5.3 add_convert_fusion.2
  514.6 40.9 %all-reduce = (f32[1024]{0:T(1024)}, f32[1024]{0:T(1024)}, f32[1024]{0:T(1024)}, f32[1024]{0:T(1024)}, f32[1024]{0:T(1024)}, /*index=5*/f32[1024]{0:T(1024)}) all-reduce(f32[1024]{0:T(1024)S(1)} %add.287, f32[1024]{0:T(1024)S(1)} %add.288, f32[1024]{0:T(1024)S(1)} %add.289, ...), channel_id=1, replica_groups=mesh['dp'=16,'tensor'=2] {'dp','tensor'}, use_global_device_ids=true, to_apply=%region_37.38 | all-reduce | flops 6144 | bytes 49152 | tf_op jit(solution)/shard_map/psum | solution.py:260
  558.9 61.2 %all-reduce.1 = (f32[1536]{0:T(1024)S(1)}, f32[2048]{0:T(1024)}) all-reduce(f32[1536]{0:T(1024)S(1)} %add.285, f32[2048]{0:T(1024)S(1)} %add.291), channel_id=1, replica_groups=mesh['dp'=16,'tensor'=2] {'dp'}, use_global_device_ids=true, to_apply=%region_33.34 | all-reduce | flops 3584 | bytes 28672 | tf_op jit(solution)/shard_map/psum | solution.py:259
  627.9 27.2 %reduce-scatter.35.cloned.1.call-done = bf16[2048,64]{0,1:T(8,128)(2,1)} async-done(((bf16[2048,1024]{0,1:T(8,128)(2,1)}), bf16[2048,64]{0,1:T(8,128)(2,1)}) %reduce-scatter.35.cloned.1.call-update) | async-done | bytes 262160 | tf_op jit(solution)/shard_map/reduce_scatter | solution.py:253
  656.8 67.7 %reduce-scatter.29.cloned.1.call-done = bf16[64,1536]{1,0:T(8,128)(2,1)} async-done(((bf16[1024,1536]{1,0:T(8,128)(2,1)}), bf16[64,1536]{1,0:T(8,128)(2,1)}) %reduce-scatter.29.cloned.1.call-update) | async-done | bytes 196624 | tf_op jit(solution)/shard_map/reduce_scatter | solution.py:244
  (256 shorter events, 90.7 us)
Async XLA Ops:
  7.2 49.6 %copy-start = (bf16[512,1024]{1,0:T(8,128)(2,1)S(1)}, bf16[512,1024]{1,0:T(8,128)(2,1)}, u32[]{:S(2)}) copy-start(bf16[512,1024]{1,0:T(8,128)(2,1)} %param.26) | copy-start | bytes 3145732
  7.2 8.5 %copy-start.27 = (bf16[1024,512]{1,0:T(8,128)(2,1)S(1)}, bf16[1024,512]{1,0:T(8,128)(2,1)}, u32[]{:S(2)}) copy-start(bf16[1024,512]{1,0:T(8,128)(2,1)} %param.23) | copy-start | bytes 3145732
  7.2 9.5 %copy-start.28 = (bf16[1024,512]{1,0:T(8,128)(2,1)S(1)}, bf16[1024,512]{1,0:T(8,128)(2,1)}, u32[]{:S(2)}) copy-start(bf16[1024,512]{1,0:T(8,128)(2,1)} %param.24) | copy-start | bytes 3145732
  7.2 10.7 %copy-start.54 = (bf16[512]{0:T(512)(128)(2,1)S(1)}, bf16[512]{0:T(512)(128)(2,1)}, u32[]{:S(2)}) copy-start(bf16[512]{0:T(512)(128)(2,1)} %param.25) | copy-start | bytes 3076
  7.2 10.6 %copy-start.55 = (bf16[512]{0:T(512)(128)(2,1)S(1)}, bf16[512]{0:T(512)(128)(2,1)}, u32[]{:S(2)}) copy-start(bf16[512]{0:T(512)(128)(2,1)} %param.22) | copy-start | bytes 3076
  7.2 73.3 %reduce-scatter.13.cloned.1.call-start = ((), (), s32[]{:S(2)}) async-start(), calls=%async_computation.12 | async-start | bytes 1572864 | tf_op jit(solution)/shard_map/reduce_scatter | solution.py:166
  9.7 16.0 %collective-permute-start.1 = (bf16[256,1024]{1,0:T(8,128)(2,1)}, bf16[256,1024]{1,0:T(8,128)(2,1)}, u32[]{:S(2)}, u32[]{:S(2)}) collective-permute-start(bf16[256,1024]{1,0:T(8,128)(2,1)} %get-tuple-element.177), channel_id=1, source_target_pairs={{0,1},{1,0},{2,3},{3,2},{4,5},{5,4},{6,7},{7,6},{8,9},{9,8},{10,11... | collective-permute-start | bytes 1572872 | tf_op jit(solution)/shard_map/ppermute | solution.py:153
  12.6 23.5 %collective-permute-start = (bf16[256,1024]{1,0:T(8,128)(2,1)}, bf16[256,1024]{1,0:T(8,128)(2,1)}, u32[]{:S(2)}, u32[]{:S(2)}) collective-permute-start(bf16[256,1024]{1,0:T(8,128)(2,1)} %get-tuple-element.178), channel_id=1, source_target_pairs={{0,1},{1,0},{2,3},{3,2},{4,5},{5,4},{6,7},{7,6},{8,9},{9,8},{10,11... | collective-permute-start | bytes 1572872 | tf_op jit(solution)/shard_map/ppermute | solution.py:153
  18.1 34.1 %copy-start.13 = (pred[512,512]{0,1:T(8,128)(4,1)}, pred[512,512]{0,1:T(8,128)(4,1)S(1)}, u32[]{:S(2)}) copy-start(pred[512,512]{0,1:T(8,128)(4,1)S(1)} %broadcast_compare_fusion.1) | copy-start | bytes 786436
  31.2 27.7 %copy-start.15 = (bf16[512,512]{0,1:T(8,128)(2,1)}, bf16[512,512]{0,1:T(8,128)(2,1)S(1)}, u32[]{:S(2)}) copy-start(bf16[512,512]{0,1:T(8,128)(2,1)S(1)} %copy.61) | copy-start | bytes 1572868
  31.4 27.4 %copy-start.17 = (bf16[512,512]{0,1:T(8,128)(2,1)}, bf16[512,512]{0,1:T(8,128)(2,1)S(1)}, u32[]{:S(2)}) copy-start(bf16[512,512]{0,1:T(8,128)(2,1)S(1)} %copy.60) | copy-start | bytes 1572868
  32.8 29.2 %copy-start.19 = (bf16[512,512]{0,1:T(8,128)(2,1)}, bf16[512,512]{0,1:T(8,128)(2,1)S(1)}, u32[]{:S(2)}) copy-start(bf16[512,512]{0,1:T(8,128)(2,1)S(1)} %copy.59) | copy-start | bytes 1572868
  58.5 45.2 %reduce-scatter.17.cloned.1.call-start = ((), (), s32[]{:S(2)}) async-start(), calls=%async_computation.15 | async-start | bytes 1572864 | tf_op jit(solution)/shard_map/reduce_scatter | solution.py:166
  65.9 14.6 %copy-start.1 = (bf16[2,256,1024]{2,1,0:T(8,128)(2,1)S(1)}, bf16[2,256,1024]{2,1,0:T(8,128)(2,1)}, u32[]{:S(2)}) copy-start(bf16[2,256,1024]{2,1,0:T(8,128)(2,1)} %param.18) | copy-start | bytes 3145732
  68.5 62.5 %all-gather.9.cloned.1.call-start = ((), (), s32[]{:S(2)}) async-start(), calls=%async_computation.16 | async-start | bytes 1572864 | tf_op jit(solution)/shard_map/all_gather | solution.py:172
  68.6 41.9 %copy-start.47 = (bf16[2048]{0:T(1024)(128)(2,1)S(1)}, bf16[2048]{0:T(1024)(128)(2,1)}, u32[]{:S(2)}) copy-start(bf16[2048]{0:T(1024)(128)(2,1)} %param.31) | copy-start | bytes 12292
  80.5 26.3 %copy-start.4 = (bf16[256,1024]{1,0:T(8,128)(2,1)S(1)}, bf16[256,1024]{1,0:T(8,128)(2,1)}, u32[]{:S(2)}) copy-start(bf16[256,1024]{1,0:T(8,128)(2,1)} %reduce-scatter.13.cloned.1.call-done) | copy-start | bytes 1572868
  109.5 44.8 %all-gather.7.cloned.1.call-start = ((), (), s32[]{:S(2)}) async-start(), calls=%async_computation.13 | async-start | bytes 1572864 | tf_op jit(solution)/shard_map/all_gather | solution.py:172
  110.0 93.4 %reduce-scatter.15.cloned.1.call-start = ((), (), s32[]{:S(2)}) async-start(), calls=%async_computation.14 | async-start | bytes 1572864 | tf_op jit(solution)/shard_map/reduce_scatter | solution.py:176
  154.3 25.3 %copy-start.56 = (bf16[2048,1024]{1,0:T(8,128)(2,1)S(1)}, bf16[2048,1024]{1,0:T(8,128)(2,1)}, u32[]{:S(2)}) copy-start(bf16[2048,1024]{1,0:T(8,128)(2,1)} %param.32) | copy-start | bytes 12582916
  182.9 43.6 %reduce-scatter.19.cloned.1.call-start = ((), (), s32[]{:S(2)}) async-start(), calls=%async_computation.17 | async-start | bytes 1572864 | tf_op jit(solution)/shard_map/reduce_scatter | solution.py:176
  183.0 6.5 copy-start.51
  183.0 6.5 copy-start.52
  183.0 6.5 copy-start.53
  183.0 43.5 %copy-start.5 = (bf16[256,1024]{1,0:T(8,128)(2,1)S(1)}, bf16[256,1024]{1,0:T(8,128)(2,1)}, u32[]{:S(2)}) copy-start(bf16[256,1024]{1,0:T(8,128)(2,1)} %reduce-scatter.17.cloned.1.call-done) | copy-start | bytes 1572868
  189.2 66.4 %all-gather.11.cloned.1.call-start = ((), (), s32[]{:S(2)}) async-start(), calls=%async_computation.18 | async-start | bytes 1572864 | tf_op jit(solution)/shard_map/all_gather | solution.py:186
  234.2 44.3 %all-gather.15.cloned.1.call-start = ((), (), s32[]{:S(2)}) async-start(), calls=%async_computation.22 | async-start | bytes 1572864 | tf_op jit(solution)/shard_map/all_gather | solution.py:186
  236.4 80.6 %reduce-scatter.25.cloned.1.call-start = ((), (), s32[]{:S(2)}) async-start(), calls=%async_computation.23 | async-start | bytes 1572864 | tf_op jit(solution)/shard_map/reduce_scatter | solution.py:192
  278.5 14.6 %copy-start.57 = (bf16[1024,2048]{1,0:T(8,128)(2,1)S(1)}, bf16[1024,2048]{1,0:T(8,128)(2,1)}, u32[]{:S(2)}) copy-start(bf16[1024,2048]{1,0:T(8,128)(2,1)} %param.30) | copy-start | bytes 12582916
  296.5 43.0 %reduce-scatter.21.cloned.1.call-start = ((), (), s32[]{:S(2)}) async-start(), calls=%async_computation.19 | async-start | bytes 1572864 | tf_op jit(solution)/shard_map/reduce_scatter | solution.py:192
  302.8 65.7 %all-gather.13.cloned.1.call-start = ((), (), s32[]{:S(2)}) async-start(), calls=%async_computation.20 | async-start | bytes 1572864 | tf_op jit(solution)/shard_map/all_gather | solution.py:202
  346.9 44.8 %all-gather.17.cloned.1.call-start = ((), (), s32[]{:S(2)}) async-start(), calls=%async_computation.24 | async-start | bytes 1572864 | tf_op jit(solution)/shard_map/all_gather | solution.py:202
  349.2 271.5 %reduce-scatter.31.cloned.1.call-start = ((), (), s32[]{:S(2)}) async-start(), calls=%async_computation.27 | async-start | bytes 1114112 | tf_op jit(solution)/shard_map/reduce_scatter | solution.py:250
  394.9 227.3 %reduce-scatter.23.cloned.1.call-start = ((), (), s32[]{:S(2)}) async-start(), calls=%async_computation.21 | async-start | bytes 1572864 | tf_op jit(solution)/shard_map/reduce_scatter | solution.py:219
  401.8 14.6 %copy-start.22 = (bf16[512,512]{0,1:T(8,128)(2,1)S(1)}, bf16[512,512]{0,1:T(8,128)(2,1)}, u32[]{:S(2)}) copy-start(bf16[512,512]{0,1:T(8,128)(2,1)} %copy.56) | copy-start | bytes 1572868
  430.7 6.6 copy-start.32
  430.7 6.6 copy-start.34
  430.7 6.6 copy-start.45
  440.2 183.6 %reduce-scatter.27.cloned.1.call-start = ((), (), s32[]{:S(2)}) async-start(), calls=%async_computation.25 | async-start | bytes 1572864 | tf_op jit(solution)/shard_map/reduce_scatter | solution.py:219
  446.5 13.3 %copy-start.18 = (bf16[512,512]{0,1:T(8,128)(2,1)S(1)}, bf16[512,512]{0,1:T(8,128)(2,1)}, u32[]{:S(2)}) copy-start(bf16[512,512]{0,1:T(8,128)(2,1)} %copy-done.17) | copy-start | bytes 1572868
  459.8 19.5 %copy-start.38 = (bf16[8,64,512]{2,1,0:T(8,128)(2,1)}, bf16[8,64,512]{2,1,0:T(8,128)(2,1)S(1)}, u32[]{:S(2)}) copy-start(bf16[8,64,512]{2,1,0:T(8,128)(2,1)S(1)} %fusion.74) | copy-start | bytes 1572868
  459.8 13.7 %copy-start.44 = (bf16[512,512]{0,1:T(8,128)(2,1)S(1)}, bf16[512,512]{0,1:T(8,128)(2,1)}, u32[]{:S(2)}) copy-start(bf16[512,512]{0,1:T(8,128)(2,1)} %copy-done.43) | copy-start | bytes 1572868
  473.5 5.8 copy-start.40
  473.5 5.8 copy-start.46
  482.3 143.8 %reduce-scatter.33.cloned.1.call-start = ((), (), s32[]{:S(2)}) async-start(), calls=%async_computation.28 | async-start | bytes 4456448 | tf_op jit(solution)/shard_map/reduce_scatter | solution.py:247
  491.6 163.4 %reduce-scatter.35.cloned.1.call-start = ((), (), s32[]{:S(2)}) async-start(), calls=%async_computation.29 | async-start | bytes 4456448 | tf_op jit(solution)/shard_map/reduce_scatter | solution.py:253
  501.8 222.7 %reduce-scatter.29.cloned.1.call-start = ((), (), s32[]{:S(2)}) async-start(), calls=%async_computation.26 | async-start | bytes 3342336 | tf_op jit(solution)/shard_map/reduce_scatter | solution.py:244
  512.0 111.8 %copy-start.11 = (f32[256,1024]{1,0:T(8,128)S(1)}, f32[256,1024]{1,0:T(8,128)}, u32[]{:S(2)}) copy-start(f32[256,1024]{1,0:T(8,128)} %get-tuple-element.166) | copy-start | bytes 3145732
  (37 other events, 113.5 us)
Sparse Core Ops, SparseCore 0:
  58.7 21.7 reduce-scatter.12
  83.4 20.3 reduce-scatter.16
  109.6 21.3 all-gather.8
  132.9 21.2 all-gather.6
  183.0 20.3 reduce-scatter.14
  206.2 20.3 reduce-scatter.18
  234.3 21.2 all-gather.10
  257.2 21.2 all-gather.14
  296.6 20.3 reduce-scatter.24
  319.1 20.3 reduce-scatter.20
  347.1 21.2 all-gather.12
  370.4 21.2 all-gather.16
  395.3 57.3 reduce-scatter.30
  455.0 19.3 reduce-scatter.22
  482.4 20.5 reduce-scatter.26
  507.2 72.8 reduce-scatter.32
  583.8 71.2 reduce-scatter.34
  659.2 65.2 reduce-scatter.28
